TPU v7x, 256 devices: a whole 4x4x8 slice. The times are simulated.
256 devices in a mesh: lon: 64 (over x_hi, z, y), lat: 4 (over x_lo, core).
Axes of the slice: x: 4 (x_hi: 2, x_lo: 2; x = x_hi * 2 + x_lo), y: 4, z: 8, core: 2. Of those that a mesh axis runs over, the one named last changes fastest.
Arguments:
- height: float32 [256, 16000], P('lat', 'lon'), may hold values from -6 to 6
- divergence: float32 [256, 16000], P('lat', 'lon'), may hold values from -6 to 6
- depth: float32 [256, 16000], P('lat', 'lon'), may hold values from 0.25 to 4
- tide: float32 [256, 16000], P('lat', 'lon'), may hold values from -6 to 6
- gauss_weight: float32 [128], P('lat'), may hold values from 0.5 to 1.5
- legendre: bfloat16 [1792, 128, 3585], P('lon', 'lat'), may hold values from -4 to 4
Outputs:
- height_new: float32 [256, 16000], P('lat', 'lon')
- divergence_new: float32 [256, 16000], P('lat', 'lon')
All inputs are finite; a program needn't handle non-finite values.
Results may differ from a plain program's by a relative error of at most 0.0032.
Values may be sent and summed in bfloat16 or wider, within the bound.
A program may use at most 128 MiB of HBM per device.

v0:
```python
import math
import jax
import jax.numpy as jnp
from jax import lax
from jax.sharding import PartitionSpec as P

time_step = 0.5
drag_step = 0.1
coupling = 2.0
gravity_step = 4.0
section_length = 128
highest = lax.Precision.HIGHEST


def angle_table(first_index, second, period):
    product = first_index[:, None] * second[None, :] % period
    angle_value = product.astype(jnp.float32) * (2.0 * math.pi / period)
    return (jnp.cos(angle_value), jnp.sin(angle_value))


def slot_layout(pair_first, pair_count, wave_count, slot_count):
    pair_index = pair_first + jnp.arange(pair_count, dtype=jnp.int32)
    slot_index = jnp.arange(slot_count, dtype=jnp.int32)[None, :]
    pair_column = pair_index[:, None]
    upper_slot = slot_index >= wave_count - pair_column
    degree = jnp.where(upper_slot, slot_index - 1, pair_column + slot_index)
    parity = jnp.where(upper_slot, (slot_index + pair_column + wave_count) % 2, slot_index % 2)
    eigen_value = (
        degree.astype(jnp.float32)
        * (degree + 1).astype(jnp.float32)
        / float(wave_count * wave_count)
    )
    return (upper_slot, parity, eigen_value)


def helmholtz(height_rhs, div_rhs, eigen_value):
    height_spec = (height_rhs - time_step * div_rhs) / (1.0 + coupling * eigen_value)
    div_spec = div_rhs + gravity_step * eigen_value * height_spec
    return jnp.stack([height_spec, div_spec]).astype(jnp.bfloat16)


def forward_fourier(row_block, wave_count, lon_groups):
    item_count, row_count, lon_total = row_block.shape
    inner_count = lon_total // section_length
    outer_count = -(-wave_count // section_length)
    flat_rows = row_block.reshape(item_count * row_count, section_length, inner_count)
    section_index = jnp.arange(section_length, dtype=jnp.int32)
    inner_index = jnp.arange(inner_count, dtype=jnp.int32)
    outer_index = jnp.arange(outer_count, dtype=jnp.int32)
    first_cos, first_sin = angle_table(section_index, section_index, section_length)
    section_real = jnp.einsum("qab,ak->qkb", flat_rows, first_cos, precision=highest)
    section_imag = -jnp.einsum("qab,ak->qkb", flat_rows, first_sin, precision=highest)
    twist_cos, twist_sin = angle_table(section_index, inner_index, lon_total)
    turned_real = section_real * twist_cos + section_imag * twist_sin
    turned_imag = section_imag * twist_cos - section_real * twist_sin
    second_cos, second_sin = angle_table(inner_index, outer_index, inner_count)
    wave_real = jnp.einsum("qkb,bt->qtk", turned_real, second_cos, precision=highest) + jnp.einsum(
        "qkb,bt->qtk", turned_imag, second_sin, precision=highest
    )
    wave_imag = jnp.einsum("qkb,bt->qtk", turned_imag, second_cos, precision=highest) - jnp.einsum(
        "qkb,bt->qtk", turned_real, second_sin, precision=highest
    )
    lon_scale = 1.0 / lon_total
    wave_real = wave_real.reshape(item_count * row_count, outer_count * section_length) * lon_scale
    wave_imag = wave_imag.reshape(item_count * row_count, outer_count * section_length) * lon_scale
    half_count = wave_count // 2
    pair_count = half_count // lon_groups

    def arrange(values):
        lower_part = values[:, :half_count].reshape(-1, lon_groups, pair_count)
        upper_part = values[:, half_count:][:, ::-1].reshape(-1, lon_groups, pair_count)
        return jnp.stack([lower_part, upper_part], axis=2)

    packed = jnp.stack([arrange(wave_real), arrange(wave_imag)], axis=2)
    return packed.reshape(item_count, row_count, lon_groups * 4 * pair_count)


def inverse_fourier(packed, wave_count, lon_groups, lon_total):
    item_count, row_count, width_count = packed.shape
    half_count = wave_count // 2
    pair_count = half_count // lon_groups
    split_form = packed.reshape(item_count * row_count, lon_groups, 2, 2, pair_count)
    lower_part = jnp.transpose(split_form[:, :, :, 0], (0, 2, 1, 3)).reshape(-1, 2, half_count)
    upper_part = jnp.transpose(split_form[:, :, :, 1], (0, 2, 1, 3)).reshape(-1, 2, half_count)[
        :, :, ::-1
    ]
    ordered = jnp.concatenate([lower_part, upper_part], axis=2)
    wave_index = jnp.arange(wave_count, dtype=jnp.int32)
    factor = jnp.where(wave_index == 0, 1.0, 2.0).astype(jnp.float32)
    inner_count = lon_total // section_length
    outer_count = -(-wave_count // section_length)
    coef_real = (ordered[:, 0] * factor).reshape(-1, outer_count, section_length)
    coef_imag = (ordered[:, 1] * factor).reshape(-1, outer_count, section_length)
    section_index = jnp.arange(section_length, dtype=jnp.int32)
    inner_index = jnp.arange(inner_count, dtype=jnp.int32)
    outer_index = jnp.arange(outer_count, dtype=jnp.int32)
    second_cos, second_sin = angle_table(outer_index, inner_index, inner_count)
    part_real = jnp.einsum("qtk,tb->qkb", coef_real, second_cos, precision=highest) - jnp.einsum(
        "qtk,tb->qkb", coef_imag, second_sin, precision=highest
    )
    part_imag = jnp.einsum("qtk,tb->qkb", coef_real, second_sin, precision=highest) + jnp.einsum(
        "qtk,tb->qkb", coef_imag, second_cos, precision=highest
    )
    twist_cos, twist_sin = angle_table(section_index, inner_index, lon_total)
    turned_real = part_real * twist_cos - part_imag * twist_sin
    turned_imag = part_real * twist_sin + part_imag * twist_cos
    first_cos, first_sin = angle_table(section_index, section_index, section_length)
    grid_rows = jnp.einsum("qkb,ak->qab", turned_real, first_cos, precision=highest) - jnp.einsum(
        "qkb,ak->qab", turned_imag, first_sin, precision=highest
    )
    return grid_rows.reshape(item_count, row_count, lon_total)


def per_device(height, divergence, depth, tide, gauss_weight, legendre):
    lon_groups = lax.axis_size("lon")
    lat_groups = lax.axis_size("lat")
    pair_count, north_count, slot_count = legendre.shape
    wave_count = 2 * pair_count * lon_groups
    lat_count = 2 * north_count * lat_groups
    lon_total = height.shape[1] * lon_groups
    norm_factor = math.sqrt(lon_total / lat_count) / wave_count
    forcing = jnp.stack(
        [
            height - time_step * (depth - 1.0) * divergence,
            divergence * (1.0 - drag_step / depth),
            tide,
        ]
    )
    spread = forward_fourier(
        lax.all_to_all(forcing, "lon", split_axis=1, concat_axis=2, tiled=True),
        wave_count,
        lon_groups,
    )
    band_waves = lax.all_to_all(spread, "lon", split_axis=2, concat_axis=1, tiled=True)
    band_form = band_waves.reshape(3, 2, north_count, 2, 2, pair_count)
    weight = (gauss_weight * norm_factor)[None, :, None, None, None]
    even_part = (band_form[:, 0] + band_form[:, 1]) * weight
    odd_part = (band_form[:, 0] - band_form[:, 1]) * weight
    folded = jnp.stack([even_part, odd_part], axis=1).astype(jnp.bfloat16)
    lat_sums = jnp.einsum(
        "ijk,fqjrai->afqrik", legendre, folded, preferred_element_type=jnp.float32
    )
    upper_slot, parity, eigen_value = slot_layout(
        lax.axis_index("lon") * pair_count, pair_count, wave_count, slot_count
    )
    odd_slot = parity == 1
    lower_slot = jnp.logical_not(upper_slot)
    even_slot = jnp.logical_not(odd_slot)
    select_masks = jnp.stack(
        [
            jnp.stack([lower_slot & even_slot, lower_slot & odd_slot]),
            jnp.stack([upper_slot & even_slot, upper_slot & odd_slot]),
        ]
    ).astype(jnp.float32)
    spectral = jnp.einsum("aqik,afqrik->frik", select_masks, lat_sums, precision=highest)
    summed = lax.psum(spectral, "lat")
    div_rhs = summed[1] - gravity_step * eigen_value * summed[2]
    solved = helmholtz(summed[0], div_rhs, eigen_value)
    member_masks = jnp.stack([lower_slot, upper_slot]).astype(jnp.bfloat16)
    parity_masks = jnp.stack([even_slot, odd_slot]).astype(jnp.bfloat16)
    masked = (
        solved[None, None] * member_masks[:, None, None, None] * parity_masks[None, :, None, None]
    )
    slot_sums = jnp.einsum(
        "ijk,aqfrik->fqjrai", legendre, masked, preferred_element_type=jnp.float32
    )
    north_part = slot_sums[:, 0] + slot_sums[:, 1]
    south_part = slot_sums[:, 0] - slot_sums[:, 1]
    grid_waves = jnp.stack([north_part, south_part], axis=1).reshape(
        2, 2 * north_count, 4 * pair_count
    )
    lon_rows = inverse_fourier(
        lax.all_to_all(grid_waves, "lon", split_axis=1, concat_axis=2, tiled=True),
        wave_count,
        lon_groups,
        lon_total,
    )
    new_fields = lax.all_to_all(lon_rows, "lon", split_axis=2, concat_axis=1, tiled=True)
    return (new_fields[0], new_fields[1])


def solution(mesh):
    in_specs = (
        P("lat", "lon"),
        P("lat", "lon"),
        P("lat", "lon"),
        P("lat", "lon"),
        P("lat"),
        P("lon", "lat", None),
    )
    out_specs = (P("lat", "lon"), P("lat", "lon"))
    return jax.shard_map(
        per_device, mesh=mesh, in_specs=in_specs, out_specs=out_specs, check_vma=False
    )
```

profile of v0, /device:TPU:8, one launch (start us, length us, event | category | flops | bytes accessed | tf_op | source)
XLA Modules:
  0.0 645.9 jit_solution(13168154059006172092)
XLA Ops:
  7.2 0.9 stack.74
  8.1 0.9 multiply_subtract_fusion.1
  9.1 0.9 pad_maximum_fusion.1
  10.0 14.6 %all-to-all-start = ((f32[3,64,250]{2,0,1:T(4,128)}), f32[3,64,250]{2,0,1:T(4,128)S(1)}, u32[]{:S(2)}, u32[]{:S(2)}) async-start(f32[3,64,250]{2,0,1:T(4,128)} %pad_maximum_fusion.1), calls=%async_computation | async-start | bytes 524288 | tf_op jit(solution)/shard_map/all_to_all | solution.py:130
  24.6 2.9 not_and_fusion.1
  27.5 3.0 not_and_fusion.2
  30.5 1.0 add_bitcast_fusion.1
  31.5 1.0 add_bitcast_fusion.2
  32.5 0.9 fusion.5
  33.4 0.9 copy.91
  34.5 3.9 all-to-all-done
  38.5 0.6 convolution_negate_fusion
  39.1 0.6 fusion.47
  41.1 1.2 rev.10
  42.9 1.2 rev.9
  45.7 0.6 reshape.830
  46.3 5.7 copy.65
  52.5 34.1 %reduce.10 = f32[7168,3]{1,0:T(8,128)} reduce(f32[7168,1,3]{2,1,0:T(1,128)} %bitcast.112, f32[]{:T(128)} %broadcast.873), dimensions={1}, to_apply=%bitcast.101.reduce_sub_computation | reduce | bytes 172036
  86.5 4.3 reshape.853
  90.8 8.9 %all-to-all-start.1 = ((f32[64,1,336]{2,1,0:T(1,128)}), f32[64,1,336]{2,1,0:T(1,128)S(1)}, u32[]{:S(2)}, u32[]{:S(2)}) async-start(f32[64,1,336]{2,1,0:T(1,128)} %reshape.853), calls=%async_computation.1 | async-start | bytes 196608 | tf_op jit(solution)/shard_map/all_to_all | solution.py:134
  99.8 11.4 %all-to-all-done.1 = f32[64,1,336]{2,1,0:T(1,128)S(1)} async-done(((f32[64,1,336]{2,1,0:T(1,128)}), f32[64,1,336]{2,1,0:T(1,128)S(1)}, u32[]{:S(2)}, u32[]{:S(2)}) %all-to-all-start.1) | async-done | bytes 86048 | tf_op jit(solution)/shard_map/all_to_all | solution.py:134
  111.3 0.9 reduce.11
  112.1 6.9 %reshape.854 = f32[7168,1,3]{2,1,0:T(1,128)} reshape(f32[64,336]{1,0:T(8,128)S(1)} %reduce.11) | data formatting | bytes 172032
  119.0 7.1 %copy.66 = f32[3,1,7168]{2,0,1:T(4,128)S(1)} copy(f32[3,1,7168]{0,1,2:T(1,128)} %bitcast.111) | data formatting | bytes 172032 | tf_op jit(solution)/shard_map/all_to_all | solution.py:134
  126.1 0.7 reshape.831
  127.5 19.9 %fusion = f32[28,3585,3,2]{1,3,2,0:T(2,128)} fusion(bf16[28,32,3585]{2,1,0:T(8,128)(2,1)} %param.11, f32[28,3585,2,2]{1,2,3,0:T(2,128)S(1)} %copy.91, bf16[3,1,32,2,2,28]{2,4,3,1,0,5:T(2,128)(2,1)S(1)} %get-tuple-element.17, bf16[3,1,32,2,2,28]{2,4,3,1,0,5:T(2,128)(2,1)S(1)} %get-tuple-element.16), kind=kOutput, calls=%fused_computation.1 | convolution fusion | flops 158485664 | bytes 10482528 | tf_op jit(solution)/shard_map/ijk,fqjrai->afqrik/dot_general | solution.py:140
  147.4 2.0 add_convert_fusion.1
  149.4 1.0 add_convert_fusion
  150.7 59.3 %all-reduce.2.cloned.1.call-done = f32[3,2,28,3585]{3,1,0,2:T(2,128)} async-done(((f32[3,2,28,3585]{3,1,0,2:T(2,128)}), f32[3,2,28,3585]{3,1,0,2:T(2,128)}) %all-reduce.2.cloned.1.call-update) | async-done | bytes 2409136 | tf_op jit(solution)/shard_map/psum | solution.py:156
  210.0 2.7 fusion.182
  212.6 0.8 add_convert_fusion.2
  213.4 1.1 pad_maximum_fusion
  214.6 1.8 broadcast_multiply_fusion
  216.4 7.6 %fusion.8 = f32[2,2,32,2,2,28]{2,3,0,1,4,5:T(2,128)S(1)} fusion(bf16[28,32,3585]{2,1,0:T(8,128)(2,1)} %param.11, bf16[2,28,3585]{2,0,1:T(2,128)(2,1)S(1)} %add_convert_fusion.1, bf16[2,2,2,28,3585]{4,2,1,0,3:T(2,128)(2,1)S(1)} %broadcast_multiply_fusion), kind=kOutput, calls=%fused_computation.19 | convolution fusion | flops 109213440 | bytes 8489264 | tf_op jit(solution)/shard_map/ijk,aqfrik->fqjrai/dot_general | solution.py:164
  224.5 0.9 reshape.848
  225.4 12.8 %all-to-all-start.2 = ((f32[2,64,112]{2,0,1:T(2,128)}), f32[2,64,112]{2,0,1:T(2,128)S(1)}, u32[]{:S(2)}, u32[]{:S(2)}) async-start(f32[2,64,112]{2,0,1:T(2,128)} %reshape.848), calls=%async_computation.2 | async-start | bytes 131072 | tf_op jit(solution)/shard_map/all_to_all | solution.py:173
  238.3 11.3 %all-to-all-done.2 = f32[2,64,112]{2,0,1:T(2,128)S(1)} async-done(((f32[2,64,112]{2,0,1:T(2,128)}), f32[2,64,112]{2,0,1:T(2,128)S(1)}, u32[]{:S(2)}, u32[]{:S(2)}) %all-to-all-start.2) | async-done | bytes 57376 | tf_op jit(solution)/shard_map/all_to_all | solution.py:173
  250.2 1.3 rev.11
  253.9 0.5 fusion.13
  254.7 11.8 %copy.74 = f32[2,1,16000]{0,1,2:T(1,128)} copy(f32[2,1,16000]{2,0,1:T(2,128)S(1)} %reshape.836) | data formatting | bytes 256000 | tf_op jit(solution)/shard_map/reshape | solution.py:111
  266.5 72.8 %reduce.12 = f32[16000,2]{1,0:T(8,128)} reduce(f32[16000,1,2]{2,1,0:T(1,128)} %bitcast.110, f32[]{:T(128)} %broadcast.873), dimensions={1}, to_apply=%bitcast.103.reduce_sub_computation | reduce | bytes 256004
  339.3 6.7 %reshape.855 = f32[64,1,500]{2,1,0:T(1,128)S(1)} reshape(f32[16000,2]{1,0:T(8,128)} %reduce.12) | data formatting | bytes 256000
  346.0 16.7 %all_to_all.16 = f32[64,1,500]{2,1,0:T(1,128)S(1)} all-to-all(f32[64,1,500]{2,1,0:T(1,128)S(1)} %reshape.855), channel_id=1, replica_groups=mesh['lon'=64,'lat'=4] {'lon'}, dimensions={0} | all-to-all | bytes 256000 | tf_op jit(solution)/shard_map/all_to_all | solution.py:178
  362.7 1.0 reduce.13
  363.6 10.4 %reshape.856 = f32[16000,1,2]{2,1,0:T(1,128)} reshape(f32[64,500]{1,0:T(8,128)S(1)} %reduce.13) | data formatting | bytes 256000
  374.1 263.0 %slice_reduce_fusion = (f32[16000]{0:T(1024)S(1)}, f32[16000]{0:T(1024)S(1)}) fusion(f32[2,1,16000]{0,1,2:T(1,128)} %bitcast.109), kind=kLoop, calls=%fused_computation.2 | loop fusion | bytes 256000 | tf_op jit(solution)/shard_map/slice | solution.py:179
  637.0 0.8 squeeze.34
  637.9 0.8 squeeze.16
  (62 shorter events, 9.1 us)
Async XLA Ops:
  10.0 28.4 %all-to-all-start = ((f32[3,64,250]{2,0,1:T(4,128)}), f32[3,64,250]{2,0,1:T(4,128)S(1)}, u32[]{:S(2)}, u32[]{:S(2)}) async-start(f32[3,64,250]{2,0,1:T(4,128)} %pad_maximum_fusion.1), calls=%async_computation | async-start | bytes 524288 | tf_op jit(solution)/shard_map/all_to_all | solution.py:130
  86.5 13.3 %copy-start.2 = (f32[32]{0:T(128)S(1)}, f32[32]{0:T(128)}, u32[]{:S(2)}) copy-start(f32[32]{0:T(128)} %param.10) | copy-start | bytes 388
  90.8 20.4 %all-to-all-start.1 = ((f32[64,1,336]{2,1,0:T(1,128)}), f32[64,1,336]{2,1,0:T(1,128)S(1)}, u32[]{:S(2)}, u32[]{:S(2)}) async-start(f32[64,1,336]{2,1,0:T(1,128)} %reshape.853), calls=%async_computation.1 | async-start | bytes 196608 | tf_op jit(solution)/shard_map/all_to_all | solution.py:134
  99.8 110.2 %all-reduce.2.cloned.1.call-start = ((), (), s32[]{:S(2)}) async-start(), calls=%async_computation.4 | async-start | bytes 4988928 | tf_op jit(solution)/shard_map/psum | solution.py:156
  147.4 2.1 copy-start.1
  209.9 2.7 copy-start
  225.4 24.1 %all-to-all-start.2 = ((f32[2,64,112]{2,0,1:T(2,128)}), f32[2,64,112]{2,0,1:T(2,128)S(1)}, u32[]{:S(2)}, u32[]{:S(2)}) async-start(f32[2,64,112]{2,0,1:T(2,128)} %reshape.848), calls=%async_computation.2 | async-start | bytes 131072 | tf_op jit(solution)/shard_map/all_to_all | solution.py:173
Sparse Core Ops, SparseCore 0:
  147.5 62.3 all-reduce.1
where the time goes:
time: 656 us; the launch traced here: 646 us
  local copies, waits for them, and re-layouts  329 us (50%)
  other arithmetic  130 us (20%)
  waiting for transfers between devices  85.8 us (13%)
  starting transfers between devices  36.4 us (6%)
  matrix products  33.1 us (5%)
  blocking collectives  16.7 us (3%)
  between operations  14.9 us (2%)
    slice x1, local copies, waits for them, and re-layouts, per_device(): return (new_fields[0], new_fields[1])  263 us
    unnamed x3, other arithmetic  108 us
    psum x1, waiting for transfers between devices, per_device(): summed = lax.psum(spectral, 'lat')  59.3 us
    unnamed x16, local copies, waits for them, and re-layouts  30.1 us
    dot_general x1, matrix products, per_device(): jnp.einsum('ijk,fqjrai->afqrik', legendre, folded, preferred_element_type...  19.9 us
    all_to_all x1, blocking collectives, per_device(): lax.all_to_all(lon_rows, 'lon', split_axis=2, concat_axis=1, tiled=True)  16.7 us
    all_to_all x1, starting transfers between devices, per_device(): lax.all_to_all(forcing, 'lon', split_axis=1, concat_axis=2, tiled=True)  14.6 us
  transfers between devices with their start and end apart: 4, of which 4 were waited for; matrix products, arithmetic and copies ran while one was open for 2% of the time, Pallas kernels for 0%

commit v1 on v0

--- a/solution.py
+++ b/solution.py
@@ -153,7 +153,7 @@
         ]
     ).astype(jnp.float32)
     spectral = jnp.einsum("aqik,afqrik->frik", select_masks, lat_sums, precision=highest)
-    summed = lax.psum(spectral, "lat")
+    summed = jnp.sum(lax.all_gather(spectral, "lat"), axis=0)
     div_rhs = summed[1] - gravity_step * eigen_value * summed[2]
     solved = helmholtz(summed[0], div_rhs, eigen_value)
     member_masks = jnp.stack([lower_slot, upper_slot]).astype(jnp.bfloat16)

time: 656 us -> 701 us (1.069)
  waiting for transfers between devices: 85.8 us -> 111 us
  other arithmetic: 130 us -> 145 us
    all_gather x0 -> x1, waiting for transfers between devices: none -> 84.5 us  [per_device(): summed = jnp.sum(lax.all_gather(spectral, 'lat'), axis=0)]
    psum x1 -> x0, waiting for transfers between devices: 59.3 us -> none  [per_device(): summed = lax.psum(spectral, 'lat')]
    reduce_sum x0 -> x1, other arithmetic: none -> 13.5 us  [per_device(): summed = jnp.sum(lax.all_gather(spectral, 'lat'), axis=0)]
    unnamed x16 -> x20, local copies, waits for them, and re-layouts: 30.1 us -> 30.1 us
where the time goes in v1:
time: 701 us; the launch traced here: 690 us
  local copies, waits for them, and re-layouts  333 us (48%)
  other arithmetic  145 us (21%)
  waiting for transfers between devices  111 us (16%)
  starting transfers between devices  36.6 us (5%)
  matrix products  33.1 us (5%)
  blocking collectives  17.2 us (2%)
  between operations  15 us (2%)
    slice x1, local copies, waits for them, and re-layouts, per_device(): return (new_fields[0], new_fields[1])  263 us
    unnamed x3, other arithmetic  108 us
    all_gather x1, waiting for transfers between devices, per_device(): summed = jnp.sum(lax.all_gather(spectral, 'lat'), axis=0)  84.5 us
    unnamed x20, local copies, waits for them, and re-layouts  30.1 us
    dot_general x1, matrix products, per_device(): jnp.einsum('ijk,fqjrai->afqrik', legendre, folded, preferred_element_type...  19.9 us
    all_to_all x1, blocking collectives, per_device(): lax.all_to_all(lon_rows, 'lon', split_axis=2, concat_axis=1, tiled=True)  17.2 us
    all_to_all x1, starting transfers between devices, per_device(): lax.all_to_all(forcing, 'lon', split_axis=1, concat_axis=2, tiled=True)  14.6 us
  transfers between devices with their start and end apart: 4, of which 4 were waited for; matrix products, arithmetic and copies ran while one was open for 2% of the time, Pallas kernels for 0%

profile of v1, /device:TPU:8, one launch (start us, length us, event | category | flops | bytes accessed | tf_op | source)
XLA Modules:
  0.0 690.4 jit_solution(5797792519826307311)
XLA Ops:
  7.2 0.9 stack.74
  8.1 0.9 multiply_subtract_fusion.1
  9.1 0.9 pad_maximum_fusion.1
  10.0 14.6 %all-to-all-start = ((f32[3,64,250]{2,0,1:T(4,128)}), f32[3,64,250]{2,0,1:T(4,128)S(1)}, u32[]{:S(2)}, u32[]{:S(2)}) async-start(f32[3,64,250]{2,0,1:T(4,128)} %pad_maximum_fusion.1), calls=%async_computation | async-start | bytes 524288 | tf_op jit(solution)/shard_map/all_to_all | solution.py:130
  24.6 2.9 not_and_fusion.1
  27.5 3.1 not_and_fusion.2
  30.5 1.0 add_bitcast_fusion.1
  31.5 1.0 add_bitcast_fusion.2
  32.5 0.9 fusion.5
  33.4 0.9 copy.95
  34.5 3.9 all-to-all-done
  38.5 0.6 convolution_negate_fusion
  39.1 0.6 fusion.47
  41.1 1.2 rev.10
  42.8 1.2 rev.9
  46.3 5.7 copy.67
  52.4 34.1 %reduce.10 = f32[7168,3]{1,0:T(8,128)} reduce(f32[7168,1,3]{2,1,0:T(1,128)} %bitcast.115, f32[]{:T(128)} %broadcast.873), dimensions={1}, to_apply=%bitcast.103.reduce_sub_computation | reduce | bytes 172036
  86.5 4.3 reshape.854
  90.8 9.0 %all-to-all-start.1 = ((f32[64,1,336]{2,1,0:T(1,128)}), f32[64,1,336]{2,1,0:T(1,128)S(1)}, u32[]{:S(2)}, u32[]{:S(2)}) async-start(f32[64,1,336]{2,1,0:T(1,128)} %reshape.854), calls=%async_computation.1 | async-start | bytes 196608 | tf_op jit(solution)/shard_map/all_to_all | solution.py:134
  99.9 11.4 %all-to-all-done.1 = f32[64,1,336]{2,1,0:T(1,128)S(1)} async-done(((f32[64,1,336]{2,1,0:T(1,128)}), f32[64,1,336]{2,1,0:T(1,128)S(1)}, u32[]{:S(2)}, u32[]{:S(2)}) %all-to-all-start.1) | async-done | bytes 86048 | tf_op jit(solution)/shard_map/all_to_all | solution.py:134
  111.3 0.9 reduce.11
  112.1 6.9 reshape.855
  119.0 7.1 %copy.68 = f32[3,1,7168]{2,0,1:T(4,128)S(1)} copy(f32[3,1,7168]{0,1,2:T(1,128)} %bitcast.114) | data formatting | bytes 172032 | tf_op jit(solution)/shard_map/all_to_all | solution.py:134
  126.1 0.7 reshape.831
  127.5 19.9 %fusion = f32[28,3585,3,2]{1,3,2,0:T(2,128)} fusion(bf16[28,32,3585]{2,1,0:T(8,128)(2,1)} %param.11, f32[28,3585,2,2]{1,2,3,0:T(2,128)S(1)} %copy.95, bf16[3,1,32,2,2,28]{2,4,3,1,0,5:T(2,128)(2,1)S(1)} %get-tuple-element.17, bf16[3,1,32,2,2,28]{2,4,3,1,0,5:T(2,128)(2,1)S(1)} %get-tuple-element.16), kind=kOutput, calls=%fused_computation.1 | convolution fusion | flops 158485664 | bytes 10482528 | tf_op jit(solution)/shard_map/ijk,fqjrai->afqrik/dot_general | solution.py:140
  147.4 3.4 copy.104
  150.8 1.8 add_convert_fusion.1
  152.6 1.7 add_convert_fusion
  154.3 1.0 fusion.20
  155.3 84.5 %all-gather.3.cloned.1.call-done = f32[12,2,28,3585]{3,1,2,0:T(2,128)} async-done(((f32[3,2,28,3585]{3,1,2,0:T(2,128)}), f32[12,2,28,3585]{3,1,2,0:T(2,128)}) %all-gather.3.cloned.1.call-update) | async-done | bytes 9636496 | tf_op jit(solution)/shard_map/all_gather | solution.py:156
  239.9 13.5 %reduce_sum.9 = f32[3,2,28,3585]{3,1,2,0:T(2,128)S(1)} reduce(f32[4,3,2,28,3585]{4,2,3,1,0:T(2,128)} %bitcast.116, f32[]{:T(128)} %constant.118.clone.1), dimensions={0}, to_apply=%region_0.1 | reduce | flops 1806840 | bytes 12045604 | tf_op jit(solution)/shard_map/reduce_sum | solution.py:156
  253.4 2.5 fusion.182
  255.9 0.8 add_convert_fusion.2
  256.7 3.2 broadcast_multiply_fusion
  259.9 7.7 %fusion.8 = f32[2,2,32,2,2,28]{2,3,0,1,4,5:T(2,128)S(1)} fusion(bf16[28,32,3585]{2,1,0:T(8,128)(2,1)} %param.11, bf16[2,28,3585]{2,0,1:T(2,128)(2,1)S(1)} %copy-done.3, bf16[2,2,2,28,3585]{4,2,1,0,3:T(2,128)(2,1)S(1)} %broadcast_multiply_fusion), kind=kOutput, calls=%fused_computation.20 | convolution fusion | flops 109213440 | bytes 8489264 | tf_op jit(solution)/shard_map/ijk,aqfrik->fqjrai/dot_general | solution.py:164
  268.1 0.9 reshape.849
  269.0 13.1 %all-to-all-start.2 = ((f32[2,64,112]{2,0,1:T(2,128)}), f32[2,64,112]{2,0,1:T(2,128)S(1)}, u32[]{:S(2)}, u32[]{:S(2)}) async-start(f32[2,64,112]{2,0,1:T(2,128)} %reshape.849), calls=%async_computation.2 | async-start | bytes 131072 | tf_op jit(solution)/shard_map/all_to_all | solution.py:173
  282.0 11.1 %all-to-all-done.2 = f32[2,64,112]{2,0,1:T(2,128)S(1)} async-done(((f32[2,64,112]{2,0,1:T(2,128)}), f32[2,64,112]{2,0,1:T(2,128)S(1)}, u32[]{:S(2)}, u32[]{:S(2)}) %all-to-all-start.2) | async-done | bytes 57376 | tf_op jit(solution)/shard_map/all_to_all | solution.py:173
  293.8 1.3 rev.11
  298.3 11.8 %copy.77 = f32[2,1,16000]{0,1,2:T(1,128)} copy(f32[2,1,16000]{2,0,1:T(2,128)S(1)} %reshape.836) | data formatting | bytes 256000 | tf_op jit(solution)/shard_map/reshape | solution.py:111
  310.1 72.8 %reduce.12 = f32[16000,2]{1,0:T(8,128)} reduce(f32[16000,1,2]{2,1,0:T(1,128)} %bitcast.113, f32[]{:T(128)} %broadcast.873), dimensions={1}, to_apply=%bitcast.105.reduce_sub_computation | reduce | bytes 256004
  382.9 6.7 reshape.856
  389.6 17.2 %all_to_all.16 = f32[64,1,500]{2,1,0:T(1,128)S(1)} all-to-all(f32[64,1,500]{2,1,0:T(1,128)S(1)} %reshape.856), channel_id=1, replica_groups=mesh['lon'=64,'lat'=4] {'lon'}, dimensions={0} | all-to-all | bytes 256000 | tf_op jit(solution)/shard_map/all_to_all | solution.py:178
  406.8 1.0 reduce.13
  407.8 10.4 %reshape.857 = f32[16000,1,2]{2,1,0:T(1,128)} reshape(f32[64,500]{1,0:T(8,128)S(1)} %reduce.13) | data formatting | bytes 256000
  418.2 263.2 %slice_reduce_fusion = (f32[16000]{0:T(1024)S(1)}, f32[16000]{0:T(1024)S(1)}) fusion(f32[2,1,16000]{0,1,2:T(1,128)} %bitcast.112), kind=kLoop, calls=%fused_computation.2 | loop fusion | bytes 256000 | tf_op jit(solution)/shard_map/slice | solution.py:179
  681.4 0.8 squeeze.34
  682.3 0.8 squeeze.16
  (67 shorter events, 10.0 us)
Async XLA Ops:
  10.0 28.4 %all-to-all-start = ((f32[3,64,250]{2,0,1:T(4,128)}), f32[3,64,250]{2,0,1:T(4,128)S(1)}, u32[]{:S(2)}, u32[]{:S(2)}) async-start(f32[3,64,250]{2,0,1:T(4,128)} %pad_maximum_fusion.1), calls=%async_computation | async-start | bytes 524288 | tf_op jit(solution)/shard_map/all_to_all | solution.py:130
  86.5 13.3 %copy-start.4 = (f32[32]{0:T(128)S(1)}, f32[32]{0:T(128)}, u32[]{:S(2)}) copy-start(f32[32]{0:T(128)} %param.10) | copy-start | bytes 388
  90.8 20.4 %all-to-all-start.1 = ((f32[64,1,336]{2,1,0:T(1,128)}), f32[64,1,336]{2,1,0:T(1,128)S(1)}, u32[]{:S(2)}, u32[]{:S(2)}) async-start(f32[64,1,336]{2,1,0:T(1,128)} %reshape.854), calls=%async_computation.1 | async-start | bytes 196608 | tf_op jit(solution)/shard_map/all_to_all | solution.py:134
  99.8 140.1 %all-gather.3.cloned.1.call-start = ((), (), s32[]{:S(2)}) async-start(), calls=%async_computation.4 | async-start | bytes 12472320 | tf_op jit(solution)/shard_map/all_gather | solution.py:156
  147.4 3.4 copy-start.1
  147.4 5.2 copy-start
  253.4 3.3 copy-start.2
  255.9 4.0 copy-start.3
  269.0 24.2 %all-to-all-start.2 = ((f32[2,64,112]{2,0,1:T(2,128)}), f32[2,64,112]{2,0,1:T(2,128)S(1)}, u32[]{:S(2)}, u32[]{:S(2)}) async-start(f32[2,64,112]{2,0,1:T(2,128)} %reshape.849), calls=%async_computation.2 | async-start | bytes 131072 | tf_op jit(solution)/shard_map/all_to_all | solution.py:173
Sparse Core Ops, SparseCore 0:
  150.9 88.9 all-gather.2
